TPU v7x, 32 devices: a whole 2x2x4 slice. The times are simulated.
32 devices in a mesh: group: 2 (over y), user: 2 (over core), cand: 8 (over z, x).
Axes of the slice: x: 2, y: 2, z: 4, core: 2. Of those that a mesh axis runs over, the one named last changes fastest.
Arguments:
- history: bfloat16 [4, 1024, 1024], P(('group', 'user'), None, 'cand'), parts along dimension 0, may hold values from -6 to 6
- hist_len: int32 [4], P(('group', 'user')), parts along dimension 0, may hold values from 256 to 1024
- tile_counts: int32 [4, 8], P(('group', 'user'), 'cand'), parts along dimension 0, may hold values from 0 to 3, as said below
- cand_emb: bfloat16 [4, 3072, 1024], P(('group', 'user'), 'cand'), parts along dimension 0, may hold values from -3 to 3
- w_in: bfloat16 [1024, 4096], P(None, 'cand'), may hold values from -1 to 1
- out_gain: float32 [1024], replicated, may hold values from 0.25 to 1.75
- w_out: bfloat16 [1024, 1024], P(None, 'cand'), may hold values from -0.1875 to 0.1875
Outputs:
- cand_out: bfloat16 [4, 3072, 1024], P(('group', 'user'), 'cand'), parts along dimension 0
There are 2 independent parts, one for each index of `group`. A program takes and returns all parts, laid end to end along the dimension named above; an argument that names none is the same for every part. Nothing has to cross between parts.
Inputs may be any that keep to these rules, and one draw needn't show every extreme that they name: In each user's row of tile_counts exactly 1 entries equal 3, 2 * (1) entries are 0 and all others are 1, so that each row sums to its number of entries; which entries take which value is random.
All inputs are finite; a program needn't handle non-finite values.
Results may differ from a plain program's by a relative error of at most 0.0069.
Values may be sent and summed in bfloat16 or wider, within the bound.
A program may use at most 64 MiB of HBM per device.

v0:
```python
import math
import jax
import jax.numpy as jnp
from jax import lax
from jax.sharding import PartitionSpec as P

D = 1024
HEADS = 8
DH = 128
TILE = 128


def layer_norm(values):
    center = values - jnp.mean(values, axis=-1, keepdims=True)
    spread = jnp.mean(center * center, axis=-1, keepdims=True)
    return center * lax.rsqrt(spread + 1e-05)


def attend_rows(carry, kv_piece, queries, length, score_scale):
    key_count = kv_piece.shape[0]
    values = kv_piece[:, :D].reshape(key_count, HEADS, DH)
    key_heads = kv_piece[:, D:].reshape(key_count, HEADS, DH)
    scores = (
        jnp.einsum("rhe,the->hrt", queries, key_heads, preferred_element_type=jnp.float32)
        * score_scale
    )
    positions = jnp.arange(key_count, dtype=jnp.int32)
    weights = jnp.where(positions[None, None, :] < length, jax.nn.silu(scores), 0.0).astype(
        jnp.bfloat16
    )
    mixed_sum = jnp.einsum("hrt,the->rhe", weights, values, preferred_element_type=jnp.float32)
    return mixed_sum.reshape(carry.shape)


def score_rows(embedded, history, length, w_in, out_gain, w_out):
    score_scale = 1.0 / math.sqrt(DH)
    rows_here = embedded.shape[0]
    normed = layer_norm(embedded.astype(jnp.float32)).astype(jnp.bfloat16)
    initial = jnp.zeros((rows_here, D), jnp.float32)
    own_events = lax.all_to_all(history, "cand", split_axis=0, concat_axis=1, tiled=True)
    hist_normed = layer_norm(own_events.astype(jnp.float32)).astype(jnp.bfloat16)
    stacked = jnp.concatenate([normed, hist_normed], axis=0)
    projected = jax.nn.silu(
        jnp.dot(
            stacked,
            lax.all_gather(w_in, "cand", axis=1, tiled=True),
            preferred_element_type=jnp.float32,
        )
    ).astype(jnp.bfloat16)
    proj_rows = projected[:rows_here]
    hist_proj = projected[rows_here:]
    kv_local = jnp.concatenate([hist_proj[:, D : 2 * D], hist_proj[:, 3 * D :]], axis=1)
    queries = proj_rows[:, 2 * D : 3 * D].reshape(rows_here, HEADS, DH)
    summed = attend_rows(
        initial, lax.all_gather(kv_local, "cand", axis=0, tiled=True), queries, length, score_scale
    )
    gate_part = proj_rows[:, :D].astype(jnp.float32)
    cand_values = proj_rows[:, D : 2 * D].reshape(rows_here, HEADS, DH).astype(jnp.float32)
    cand_keys = proj_rows[:, 3 * D :].reshape(rows_here, HEADS, DH).astype(jnp.float32)
    own_score = jax.nn.silu(jnp.sum(queries.astype(jnp.float32) * cand_keys, axis=-1) * score_scale)
    attn = summed + (own_score[:, :, None] * cand_values).reshape(rows_here, D)
    gated = (layer_norm(attn) * out_gain[None, :] * gate_part).astype(jnp.bfloat16)
    residual = embedded.astype(jnp.float32)
    return (
        residual
        + jnp.dot(
            gated,
            lax.all_gather(w_out, "cand", axis=1, tiled=True),
            preferred_element_type=jnp.float32,
        )
    ).astype(jnp.bfloat16)


def shards(history, hist_len, tile_counts, cand_emb, w_in, out_gain, w_out):
    tile_total = tile_counts[0, 0]
    length = hist_len[0]
    slot_rows = cand_emb[0]
    slot_count = slot_rows.shape[0]
    own_history = history[0]
    scored = score_rows(slot_rows, own_history, length, w_in, out_gain, w_out)
    live = jnp.arange(slot_count, dtype=jnp.int32) < tile_total * TILE
    result = jnp.where(live[:, None], scored, jnp.zeros_like(scored))
    return result[None]


def solution(mesh):
    in_specs = (
        P(("group", "user"), None, "cand"),
        P(("group", "user")),
        P(("group", "user"), "cand"),
        P(("group", "user"), "cand", None),
        P(None, "cand"),
        P(),
        P(None, "cand"),
    )
    out_specs = P(("group", "user"), "cand", None)
    return jax.shard_map(shards, mesh=mesh, in_specs=in_specs, out_specs=out_specs, check_vma=False)
```

profile of v0, /device:TPU:0, one launch (start us, length us, event | category | flops | bytes accessed | tf_op | source)
XLA Modules:
  0.0 282.9 jit_solution(6100628635871063216)
XLA Ops:
  6.5 0.0 copy-start
  6.5 0.0 all-gather.4.cloned.1.call-start
  6.5 0.7 all-gather.4.cloned.1.call-update
  7.3 7.3 %all-to-all-start = ((bf16[8,128,128]{2,1,0:T(8,128)(2,1)}), bf16[8,128,128]{2,1,0:T(8,128)(2,1)S(1)}, u32[]{:S(2)}, u32[]{:S(2)}) async-start(bf16[8,128,128]{2,1,0:T(8,128)(2,1)} %bitcast.72), calls=%async_computation | async-start | bytes 524288 | tf_op jit(solution)/shard_map/all_to_all | solution.py:40
  14.5 0.0 all-gather.6.cloned.1.call-start
  14.6 0.0 copy-done
  14.6 0.2 convert_reduce_fusion
  14.8 0.3 fusion.11
  15.1 0.3 fusion.12
  15.4 8.1 %all-to-all-done = bf16[8,128,128]{2,1,0:T(8,128)(2,1)S(1)} async-done(((bf16[8,128,128]{2,1,0:T(8,128)(2,1)}), bf16[8,128,128]{2,1,0:T(8,128)(2,1)S(1)}, u32[]{:S(2)}, u32[]{:S(2)}) %all-to-all-start) | async-done | bytes 262176 | tf_op jit(solution)/shard_map/all_to_all | solution.py:40
  23.5 0.1 convert_reduce_fusion.1
  23.6 0.2 fusion.32
  23.8 0.2 fusion.34
  24.1 113.9 %all-gather.4.cloned.1.call-done = bf16[1024,4096]{1,0:T(8,128)(2,1)} async-done(((bf16[1024,512]{1,0:T(8,128)(2,1)}), bf16[1024,4096]{1,0:T(8,128)(2,1)}) %all-gather.4.cloned.1.call-update) | async-done | bytes 8388624 | tf_op jit(solution)/shard_map/all_gather | solution.py:46
  137.9 8.6 %multiply_convert_fusion = bf16[512,4096]{1,0:T(8,128)(2,1)S(1)} fusion(bf16[1024,4096]{1,0:T(8,128)(2,1)} %all-gather.4.cloned.1.call-done, bf16[128,1024]{1,0:T(8,128)(2,1)S(1)} %fusion.34, bf16[384,1024]{1,0:T(8,128)(2,1)S(1)} %fusion.12), kind=kOutput, calls=%fused_computation.1 | convolution fusion | flops 4307550208 | bytes 13631488 | tf_op jit(solution)/shard_map/dot_general | solution.py:44
  146.6 0.0 copy-start.2
  146.6 1.9 copy-done.2
  148.5 0.9 pad_maximum_fusion
  149.4 0.0 all-gather.6.cloned.1.call-update
  149.4 0.0 all-gather.8.cloned.1.call-start
  149.5 0.7 all-gather.8.cloned.1.call-update
  151.5 2.6 slice_bitcast_fusion.2
  154.1 0.3 copy.37
  154.4 0.2 copy.36
  154.6 0.5 multiply_reduce_fusion.1
  155.1 0.1 copy.29
  155.2 0.1 copy.30
  155.3 65.8 %all-gather.6.cloned.1.call-done = bf16[1024,2048]{1,0:T(8,128)(2,1)} async-done(((bf16[128,2048]{1,0:T(8,128)(2,1)}), bf16[1024,2048]{1,0:T(8,128)(2,1)}) %all-gather.6.cloned.1.call-update) | async-done | bytes 4194320 | tf_op jit(solution)/shard_map/all_gather | solution.py:55
  221.2 4.2 %slice_bitcast_fusion = (bf16[128,8,8,128]{3,2,1,0:T(8,128)(2,1)}, bf16[1024,1024]{1,0:T(8,128)(2,1)S(1)}) fusion(bf16[1024,2048]{1,0:T(8,128)(2,1)} %all-gather.6.cloned.1.call-done), kind=kLoop, calls=%fused_computation.6 | loop fusion | bytes 8388608
  225.4 2.6 copy.31
  227.9 7.5 %fusion = f32[8,128,384]{2,1,0:T(8,128)S(1)} fusion(bf16[1024,8,128]{0,2,1:T(8,128)(2,1)} %bitcast.70, pred[1024]{0:T(1024)(128)(4,1)S(1)} %iota_compare_fusion, bf16[128,8,8,128]{3,2,1,0:T(8,128)(2,1)} %get-tuple-element.10, bf16[48,8,8,128]{3,2,1,0:T(8,128)(2,1)} %get-tuple-element.8), kind=kOutput, calls=%fused_computation.2 | convolution fusion | flops 1632632832 | bytes 6554624 | tf_op jit(solution)/shard_map/hrt,the->rhe/dot_general | solution.py:31
  235.4 1.6 copy.32
  237.1 0.0 copy-start.1
  237.1 0.5 mul.114
  237.6 0.9 copy-done.1
  238.5 0.0 copy-start.3
  238.5 1.7 fusion.39
  240.2 0.3 multiply_reduce_fusion
  240.5 32.1 %all-gather.8.cloned.1.call-done = bf16[1024,1024]{1,0:T(8,128)(2,1)} async-done(((bf16[1024,128]{1,0:T(8,128)(2,1)}), bf16[1024,1024]{1,0:T(8,128)(2,1)}) %all-gather.8.cloned.1.call-update) | async-done | bytes 2097168 | tf_op jit(solution)/shard_map/all_gather | solution.py:68
  272.6 0.0 copy-done.3
  272.6 3.8 %fusion.16 = bf16[1,384,1024]{2,1,0:T(8,128)(2,1)} fusion(bf16[1024,1024]{1,0:T(8,128)(2,1)} %all-gather.8.cloned.1.call-done, bf16[1,384,1024]{2,1,0:T(8,128)(2,1)S(1)} %copy-done, f32[384,1024]{1,0:T(8,128)S(1)} %get-tuple-element.6, bf16[512,4096]{1,0:T(8,128)(2,1)} %copy-done.2, f32[1024]{0:T(1024)S(1)} %copy-done.3, f32[384]{0:T(512)S(1)} %add_rsqrt_fusion, ...), kind=kOutput, calls=%fused_computation.23 | convolution fusion | flops 809238528 | bytes 6036864 | tf_op jit(solution)/shard_map/dot_general | solution.py:66
  (10 shorter events, 0.1 us)
Async XLA Ops:
  6.5 8.0 %copy-start = (bf16[1,384,1024]{2,1,0:T(8,128)(2,1)S(1)}, bf16[1,384,1024]{2,1,0:T(8,128)(2,1)}, u32[]{:S(2)}) copy-start(bf16[1,384,1024]{2,1,0:T(8,128)(2,1)} %param.10) | copy-start | bytes 2359300
  6.5 131.4 %all-gather.4.cloned.1.call-start = ((), (), s32[]{:S(2)}) async-start(), calls=%async_computation.1 | async-start | bytes 9437184 | tf_op jit(solution)/shard_map/all_gather | solution.py:46
  7.3 16.2 %all-to-all-start = ((bf16[8,128,128]{2,1,0:T(8,128)(2,1)}), bf16[8,128,128]{2,1,0:T(8,128)(2,1)S(1)}, u32[]{:S(2)}, u32[]{:S(2)}) async-start(bf16[8,128,128]{2,1,0:T(8,128)(2,1)} %bitcast.72), calls=%async_computation | async-start | bytes 524288 | tf_op jit(solution)/shard_map/all_to_all | solution.py:40
  14.5 206.6 %all-gather.6.cloned.1.call-start = ((), (), s32[]{:S(2)}) async-start(), calls=%async_computation.2 | async-start | bytes 4718592 | tf_op jit(solution)/shard_map/all_gather | solution.py:55
  146.6 1.9 copy-start.2
  149.4 123.2 %all-gather.8.cloned.1.call-start = ((), (), s32[]{:S(2)}) async-start(), calls=%async_computation.3 | async-start | bytes 2359296 | tf_op jit(solution)/shard_map/all_gather | solution.py:68
  237.1 1.4 copy-start.1
  238.5 34.1 %copy-start.3 = (f32[1024]{0:T(1024)S(1)}, f32[1024]{0:T(1024)}, u32[]{:S(2)}) copy-start(f32[1024]{0:T(1024)} %param.12) | copy-start | bytes 12292
Sparse Core Ops, SparseCore 0:
  9.4 128.4 all-gather.3
  149.5 71.5 all-gather.5
  223.2 49.3 all-gather.7
where the time goes:
time: 283 us
  waiting for transfers between devices  221 us (78%)
  matrix products  19.9 us (7%)
  between operations  14.5 us (5%)
  local copies, waits for them, and re-layouts  12.5 us (4%)
  other arithmetic  7.38 us (3%)
  starting transfers between devices  7.35 us (3%)
    all_gather x1, waiting for transfers between devices, score_rows(): lax.all_gather(w_in, 'cand', axis=1, tiled=True)  114 us
    all_gather x1, waiting for transfers between devices, score_rows(): lax.all_gather(kv_local, 'cand', axis=0, tiled=True)  65.8 us
    all_gather x1, waiting for transfers between devices, score_rows(): lax.all_gather(w_out, 'cand', axis=1, tiled=True)  32.1 us
    dot_general x1, matrix products, score_rows(): jnp.dot(stacked, lax.all_gather(w_in, 'cand', axis=1, tiled=True), prefer...  8.61 us
    all_to_all x1, waiting for transfers between devices, score_rows(): lax.all_to_all(history, 'cand', split_axis=0, concat_axis=1, tiled=True)  8.08 us
    unnamed x11, local copies, waits for them, and re-layouts  7.59 us
    dot_general x1, matrix products, attend_rows(): jnp.einsum('hrt,the->rhe', weights, values, preferred_element_type=jnp.fl...  7.51 us
    all_to_all x1, starting transfers between devices, score_rows(): lax.all_to_all(history, 'cand', split_axis=0, concat_axis=1, tiled=True)  7.26 us
  transfers between devices with their start and end apart: 4, of which 4 were waited for; matrix products, arithmetic and copies ran while one was open for 8% of the time, Pallas kernels for 0%

commit v1 on v0

--- a/solution.py
+++ b/solution.py
@@ -37,7 +37,10 @@
     rows_here = embedded.shape[0]
     normed = layer_norm(embedded.astype(jnp.float32)).astype(jnp.bfloat16)
     initial = jnp.zeros((rows_here, D), jnp.float32)
-    own_events = lax.all_to_all(history, "cand", split_axis=0, concat_axis=1, tiled=True)
+    own_events = jnp.concatenate(
+        lax.all_to_all(jnp.stack(jnp.split(history, lax.axis_size("cand"), axis=0)), "cand", 0, 0),
+        axis=1,
+    )
     hist_normed = layer_norm(own_events.astype(jnp.float32)).astype(jnp.bfloat16)
     stacked = jnp.concatenate([normed, hist_normed], axis=0)
     projected = jax.nn.silu(

time: 283 us -> 292 us (1.032)
  local copies, waits for them, and re-layouts: 12.5 us -> 23.5 us
  waiting for transfers between devices: 221 us -> 218 us
    unnamed x11 -> x18, local copies, waits for them, and re-layouts: 7.59 us -> 17.2 us
    all_gather x1, waiting for transfers between devices: 114 us -> 105 us  [score_rows(): lax.all_gather(w_in, 'cand', axis=1, tiled=True)]
    all_to_all x1, waiting for transfers between devices: 8.08 us -> 13.4 us  [score_rows(): lax.all_to_all(jnp.stack(jnp.split(history, lax.axis_size('cand'), axis=0...]
  transfers between devices with their start and end apart: 4 -> 4, of which waited for: 4 -> 4; matrix products, arithmetic and copies ran while one was open for 8% -> 12% of each run, Pallas kernels for 0% -> 0%
where the time goes in v1:
time: 292 us; the launch traced here: 291 us
  waiting for transfers between devices  218 us (75%)
  local copies, waits for them, and re-layouts  23.5 us (8%)
  matrix products  19.9 us (7%)
  between operations  14.5 us (5%)
  other arithmetic  7.38 us (3%)
  starting transfers between devices  7.34 us (3%)
    all_gather x1, waiting for transfers between devices, score_rows(): lax.all_gather(w_in, 'cand', axis=1, tiled=True)  105 us
    all_gather x1, waiting for transfers between devices, score_rows(): lax.all_gather(kv_local, 'cand', axis=0, tiled=True)  65.8 us
    all_gather x1, waiting for transfers between devices, score_rows(): lax.all_gather(w_out, 'cand', axis=1, tiled=True)  32.1 us
    unnamed x18, local copies, waits for them, and re-layouts  17.2 us
    all_to_all x1, waiting for transfers between devices, score_rows(): lax.all_to_all(jnp.stack(jnp.split(history, lax.axis_size('cand'), axis=0...  13.4 us
    dot_general x1, matrix products, score_rows(): jnp.dot(stacked, lax.all_gather(w_in, 'cand', axis=1, tiled=True), prefer...  8.61 us
    dot_general x1, matrix products, attend_rows(): jnp.einsum('hrt,the->rhe', weights, values, preferred_element_type=jnp.fl...  7.5 us
    all_to_all x1, starting transfers between devices, score_rows(): lax.all_to_all(jnp.stack(jnp.split(history, lax.axis_size('cand'), axis=0...  7.26 us
  transfers between devices with their start and end apart: 4, of which 4 were waited for; matrix products, arithmetic and copies ran while one was open for 12% of the time, Pallas kernels for 0%

profile of v1, /device:TPU:0, one launch (start us, length us, event | category | flops | bytes accessed | tf_op | source)
XLA Modules:
  0.0 290.7 jit_solution(741709542393272599)
XLA Ops:
  6.5 0.0 copy-start
  6.5 0.0 all-gather.4.cloned.1.call-start
  6.5 0.7 all-gather.4.cloned.1.call-update
  7.3 1.4 slice_dynamic-update-slice_fusion.7
  8.6 1.4 slice_dynamic-update-slice_fusion.6
  10.0 1.4 slice_dynamic-update-slice_fusion.5
  11.4 1.4 slice_dynamic-update-slice_fusion.4
  12.8 1.4 slice_dynamic-update-slice_fusion.3
  14.1 1.4 slice_dynamic-update-slice_fusion.2
  15.5 1.4 slice_dynamic-update-slice_fusion.1
  16.9 1.4 slice_dynamic-update-slice_fusion
  18.3 7.3 %all-to-all-start = ((bf16[8,128,128]{2,1,0:T(8,128)(2,1)}), bf16[8,128,128]{2,1,0:T(8,128)(2,1)S(1)}, u32[]{:S(2)}, u32[]{:S(2)}) async-start(bf16[8,128,128]{2,1,0:T(8,128)(2,1)} %slice_dynamic-update-slice_fusion), calls=%async_computation | async-start | bytes 524288 | tf_op jit(solution)/shard_map/all_to_all | solution.py:41
  25.5 0.0 all-gather.6.cloned.1.call-start
  25.6 0.0 copy-done
  25.6 0.2 convert_reduce_fusion
  25.8 0.3 fusion.11
  26.1 0.3 fusion.12
  26.4 13.4 %all-to-all-done = bf16[8,128,128]{2,1,0:T(8,128)(2,1)S(1)} async-done(((bf16[8,128,128]{2,1,0:T(8,128)(2,1)}), bf16[8,128,128]{2,1,0:T(8,128)(2,1)S(1)}, u32[]{:S(2)}, u32[]{:S(2)}) %all-to-all-start) | async-done | bytes 262176 | tf_op jit(solution)/shard_map/all_to_all | solution.py:41
  39.8 0.1 convert_reduce_fusion.1
  39.9 0.2 fusion.32
  40.2 0.2 fusion.34
  40.4 105.3 %all-gather.4.cloned.1.call-done = bf16[1024,4096]{1,0:T(8,128)(2,1)} async-done(((bf16[1024,512]{1,0:T(8,128)(2,1)}), bf16[1024,4096]{1,0:T(8,128)(2,1)}) %all-gather.4.cloned.1.call-update) | async-done | bytes 8388624 | tf_op jit(solution)/shard_map/all_gather | solution.py:49
  145.7 8.6 %multiply_convert_fusion = bf16[512,4096]{1,0:T(8,128)(2,1)S(1)} fusion(bf16[1024,4096]{1,0:T(8,128)(2,1)} %all-gather.4.cloned.1.call-done, bf16[128,1024]{1,0:T(8,128)(2,1)S(1)} %fusion.34, bf16[384,1024]{1,0:T(8,128)(2,1)S(1)} %fusion.12), kind=kOutput, calls=%fused_computation.1 | convolution fusion | flops 4307550208 | bytes 13631488 | tf_op jit(solution)/shard_map/dot_general | solution.py:47
  154.3 0.0 copy-start.2
  154.3 1.9 copy-done.2
  156.3 0.9 pad_maximum_fusion
  157.1 0.0 all-gather.6.cloned.1.call-update
  157.2 0.0 all-gather.8.cloned.1.call-start
  157.2 0.7 all-gather.8.cloned.1.call-update
  159.2 2.6 slice_bitcast_fusion.2
  161.8 0.3 copy.32
  162.2 0.2 copy.31
  162.3 0.5 multiply_reduce_fusion.1
  162.8 0.1 copy.24
  163.0 0.1 copy.25
  163.1 65.8 %all-gather.6.cloned.1.call-done = bf16[1024,2048]{1,0:T(8,128)(2,1)} async-done(((bf16[128,2048]{1,0:T(8,128)(2,1)}), bf16[1024,2048]{1,0:T(8,128)(2,1)}) %all-gather.6.cloned.1.call-update) | async-done | bytes 4194320 | tf_op jit(solution)/shard_map/all_gather | solution.py:58
  228.9 4.2 %slice_bitcast_fusion = (bf16[128,8,8,128]{3,2,1,0:T(8,128)(2,1)}, bf16[1024,1024]{1,0:T(8,128)(2,1)S(1)}) fusion(bf16[1024,2048]{1,0:T(8,128)(2,1)} %all-gather.6.cloned.1.call-done), kind=kLoop, calls=%fused_computation.6 | loop fusion | bytes 8388608
  233.1 2.6 copy.26
  235.7 7.5 %fusion = f32[8,128,384]{2,1,0:T(8,128)S(1)} fusion(bf16[1024,8,128]{0,2,1:T(8,128)(2,1)} %bitcast.69, pred[1024]{0:T(1024)(128)(4,1)S(1)} %iota_compare_fusion, bf16[128,8,8,128]{3,2,1,0:T(8,128)(2,1)} %get-tuple-element.10, bf16[48,8,8,128]{3,2,1,0:T(8,128)(2,1)} %get-tuple-element.8), kind=kOutput, calls=%fused_computation.2 | convolution fusion | flops 1632632832 | bytes 6554624 | tf_op jit(solution)/shard_map/hrt,the->rhe/dot_general | solution.py:31
  243.2 1.6 copy.27
  244.8 0.5 mul.114
  245.3 0.9 copy-done.1
  246.3 0.0 copy-start.3
  246.3 1.7 fusion.39
  247.9 0.3 multiply_reduce_fusion
  248.2 32.1 %all-gather.8.cloned.1.call-done = bf16[1024,1024]{1,0:T(8,128)(2,1)} async-done(((bf16[1024,128]{1,0:T(8,128)(2,1)}), bf16[1024,1024]{1,0:T(8,128)(2,1)}) %all-gather.8.cloned.1.call-update) | async-done | bytes 2097168 | tf_op jit(solution)/shard_map/all_gather | solution.py:71
  280.4 0.0 copy-done.3
  280.4 3.8 %fusion.16 = bf16[1,384,1024]{2,1,0:T(8,128)(2,1)} fusion(bf16[1024,1024]{1,0:T(8,128)(2,1)} %all-gather.8.cloned.1.call-done, bf16[1,384,1024]{2,1,0:T(8,128)(2,1)S(1)} %copy-done, f32[384,1024]{1,0:T(8,128)S(1)} %get-tuple-element.6, bf16[512,4096]{1,0:T(8,128)(2,1)} %copy-done.2, f32[1024]{0:T(1024)S(1)} %copy-done.3, f32[384]{0:T(512)S(1)} %add_rsqrt_fusion, ...), kind=kOutput, calls=%fused_computation.23 | convolution fusion | flops 809238528 | bytes 6036864 | tf_op jit(solution)/shard_map/dot_general | solution.py:69
  (11 shorter events, 0.1 us)
Async XLA Ops:
  6.5 19.0 %copy-start = (bf16[1,384,1024]{2,1,0:T(8,128)(2,1)S(1)}, bf16[1,384,1024]{2,1,0:T(8,128)(2,1)}, u32[]{:S(2)}) copy-start(bf16[1,384,1024]{2,1,0:T(8,128)(2,1)} %param.10) | copy-start | bytes 2359300
  6.5 139.2 %all-gather.4.cloned.1.call-start = ((), (), s32[]{:S(2)}) async-start(), calls=%async_computation.1 | async-start | bytes 9437184 | tf_op jit(solution)/shard_map/all_gather | solution.py:49
  18.3 21.5 %all-to-all-start = ((bf16[8,128,128]{2,1,0:T(8,128)(2,1)}), bf16[8,128,128]{2,1,0:T(8,128)(2,1)S(1)}, u32[]{:S(2)}, u32[]{:S(2)}) async-start(bf16[8,128,128]{2,1,0:T(8,128)(2,1)} %slice_dynamic-update-slice_fusion), calls=%async_computation | async-start | bytes 524288 | tf_op jit(solution)/shard_map/all_to_all | solution.py:41
  25.5 203.4 %all-gather.6.cloned.1.call-start = ((), (), s32[]{:S(2)}) async-start(), calls=%async_computation.2 | async-start | bytes 4718592 | tf_op jit(solution)/shard_map/all_gather | solution.py:58
  154.3 1.9 copy-start.2
  157.2 123.2 %all-gather.8.cloned.1.call-start = ((), (), s32[]{:S(2)}) async-start(), calls=%async_computation.3 | async-start | bytes 2359296 | tf_op jit(solution)/shard_map/all_gather | solution.py:71
  244.8 1.4 copy-start.1
  246.3 34.1 %copy-start.3 = (f32[1024]{0:T(1024)S(1)}, f32[1024]{0:T(1024)}, u32[]{:S(2)}) copy-start(f32[1024]{0:T(1024)} %param.12) | copy-start | bytes 12292
Sparse Core Ops, SparseCore 0:
  9.4 136.2 all-gather.3
  157.3 71.5 all-gather.5
  231.0 49.3 all-gather.7
